TPU v7x, 32 devices: a whole 2x2x4 slice. The times are simulated.
32 devices in a mesh: row: 1, ang: 32 (over z, y, x, core).
Axes of the slice: x: 2, y: 2, z: 4, core: 2. Of those that a mesh axis runs over, the one named last changes fastest.
Arguments:
- linv_t: bfloat16 [2, 2048, 2048], P(None, 'ang', 'row'), may hold values from -1.5 to 1.5, as said below
- rhs_top: float32 [2, 2048, 16384], P(None, 'row', 'ang'), may hold values from -6 to 6
- factor_t: bfloat16 [2, 2048, 1024], P(None, 'ang', 'row'), may hold values from -0.125 to 0.125
- rhs_rest: float32 [2, 1024, 16384], P(None, 'row', 'ang'), may hold values from -6 to 6
Outputs:
- solved: float32 [2, 2048, 16384], P(None, 'row', 'ang')
- updated: float32 [2, 1024, 16384], P(None, 'row', 'ang')
Inputs may be any that keep to these rules, and one draw needn't show every extreme that they name: `linv_t`: lower triangular inverse: entry [c, j, i] is zero where j > i; the diagonal is real and between 0.5 and 1.5.
All inputs are finite; a program needn't handle non-finite values.
Results may differ from a plain program's by a relative error of at most 0.0026.
Values may be sent and summed in bfloat16 or wider, within the bound.
A program may use at most 128 MiB of HBM per device.

v0:
```python
import functools

import jax
import jax.numpy as jnp
from jax import lax
from jax.experimental import pallas as pl
from jax.experimental.pallas import tpu as pltpu
from jax.sharding import PartitionSpec as P

LAG = 1
KINDS = ((0, 0, "zyx"), (0, 1, "zxy"), (1, 0, "yzx"), (1, 1, "xzy"))
DIMS0 = (((0,), (0,)), ((), ()))


def tdot(first, second):
    return lax.dot_general(first, second, DIMS0, preferred_element_type=jnp.float32)


def split_two(value):
    high = value.astype(jnp.bfloat16)
    low = (value - high.astype(jnp.float32)).astype(jnp.bfloat16)
    return high, low


def general_body(linv_t, rhs_top, factor_t, rhs_rest):
    top_all = lax.all_gather(rhs_top, "row", axis=1, tiled=True)
    high, low = split_two(top_all)
    inverse = lax.all_gather(linv_t, "ang", axis=1, tiled=True)

    def single(first, second):
        return tdot(inverse[first], high[second]) + tdot(inverse[first], low[second])

    solved = jnp.stack([single(0, 0) - single(1, 1), single(0, 1) + single(1, 0)])
    half = lax.all_gather(solved.astype(jnp.bfloat16), "row", axis=1, tiled=True)
    factor = lax.all_gather(factor_t, "ang", axis=1, tiled=True)
    update = jnp.stack(
        [
            tdot(factor[0], half[0]) - tdot(factor[1], half[1]),
            tdot(factor[0], half[1]) + tdot(factor[1], half[0]),
        ]
    )
    return (solved, rhs_rest - update)


def fused_kernel(
    devices, lag, lin_ref, top_ref, fac_ref, rest_ref, solved_ref, updated_ref,
    glin, gfac, terms, acc, upd, recv, send, local,
):
    levels = devices // 8
    chips = devices // 2
    rows = lin_ref.shape[1]
    panel = lin_ref.shape[2]
    width = top_ref.shape[2]
    block = 4 * rows
    blocks = panel // block
    tail = fac_ref.shape[2] // block

    me = lax.axis_index("ang")
    core = lax.rem(me, 2)
    x = lax.rem(me // 2, 2)
    y = lax.rem(me // 4, 2)
    z = me // 8
    has_up, has_down = z < levels - 1, z > 0
    targets = (
        me + 2 - 4 * x,
        me + 4 - 8 * y,
        jnp.where(has_up, me + 8, me),
        jnp.where(has_down, me - 8, me),
        me + 1 - 2 * core,
    )
    mine = pl.ds(pl.multiple_of(me * rows, rows), rows)

    loads = (
        pltpu.make_async_copy(top_ref, acc, local.at[0]),
        pltpu.make_async_copy(lin_ref, glin.at[:, mine, :], local.at[1]),
        pltpu.make_async_copy(fac_ref, gfac.at[:, mine, :], local.at[2]),
        pltpu.make_async_copy(rest_ref, upd, local.at[3]),
    )

    barrier = pltpu.get_barrier_semaphore()

    def greet(target):
        pl.semaphore_signal(
            barrier, inc=1, device_id={"ang": target}, device_id_type=pl.DeviceIdType.MESH
        )

    for index in (0, 1, 4):
        greet(targets[index])
    pl.when(has_up)(lambda: greet(targets[2]))
    pl.when(has_down)(lambda: greet(targets[3]))
    pl.semaphore_wait(barrier, 3 + has_up.astype(jnp.int32) + has_down.astype(jnp.int32))

    def block_at(index):
        return pl.ds(pl.multiple_of(index * block, block), block)

    def place(kind, origin, cls):
        which, part, _ = KINDS[kind]
        at_rows = pl.ds(pl.multiple_of(origin * rows, rows), rows)
        if which == 0:
            return glin.at[part, at_rows, pl.ds(cls * block, panel - cls * block)]
        return gfac.at[part, at_rows, :]

    def source(kind, cls):
        which, part, _ = KINDS[kind]
        if which == 0:
            return lin_ref.at[part, :, pl.ds(cls * block, panel - cls * block)]
        return fac_ref.at[part]

    def by_class(kind, origin, action):
        if KINDS[kind][0] == 0:
            for cls in range(blocks):
                pl.when(origin // 4 == cls)(functools.partial(action, cls))
        else:
            action(0)

    def remote(kind, origin, cls, direction, own):
        return pltpu.make_async_remote_copy(
            src_ref=source(kind, cls) if own else place(kind, origin, cls),
            dst_ref=place(kind, origin, cls),
            send_sem=send.at[direction, kind, origin // 2],
            recv_sem=recv.at[kind, origin],
            device_id={"ang": targets[direction]},
            device_id_type=pl.DeviceIdType.MESH,
        )

    def onward(kind, zo, yo, xo):
        same = {"x": x == xo, "y": y == yo, "z": z == zo}
        order = KINDS[kind][2]
        free = {}
        for position, axis in enumerate(order):
            ok = True
            for later in order[position + 1 :]:
                ok = same[later] if ok is True else jnp.logical_and(ok, same[later])
            free[axis] = ok

        def both(first, second):
            return second if first is True else jnp.logical_and(first, second)

        return (
            both(free["x"], same["x"]),
            both(free["y"], same["y"]),
            both(free["z"], jnp.logical_and(z >= zo, has_up)),
            both(free["z"], jnp.logical_and(z <= zo, has_down)),
            True,
        )

    def forward(kind, origin, goes, cls, own, act):
        for direction in range(5):
            copy = remote(kind, origin, cls, direction, own)
            run = copy.start if act == "start" else copy.wait_send
            if goes[direction] is True:
                run()
            else:
                pl.when(goes[direction])(run)

    def send_own(kind):
        goes = onward(kind, z, y, x)
        by_class(kind, me, lambda cls: forward(kind, me, goes, cls, True, "start"))

    def arrive_other(kind, origin):
        by_class(kind, origin, lambda cls: remote(kind, origin, cls, 4, False).wait_recv())

    send_own(0)
    send_own(1)
    for copy in loads:
        copy.start()
    loads[0].wait()

    @pl.loop(0, blocks)
    def _(index):
        at_rows = block_at(index)
        for part in range(2):
            first, second = split_two(acc[part, at_rows, :])
            terms[pl.ds(pl.multiple_of((4 * index + 2 * part) * block, block), block), :] = first
            terms[pl.ds(pl.multiple_of((4 * index + 2 * part + 1) * block, block), block), :] = second
            acc[part, at_rows, :] = jnp.zeros((block, width), jnp.float32)

    for copy in loads[1:]:
        copy.wait()

    def solve_piece(group, index):
        at_rows, to = block_at(group), block_at(index)
        lreal, limag = glin[0, at_rows, to].T, glin[1, at_rows, to].T
        right = terms[pl.ds(pl.multiple_of(4 * group * block, block), 4 * block), :]
        real = jnp.concatenate([lreal, lreal, -limag, -limag], axis=1)
        imag = jnp.concatenate([limag, limag, lreal, lreal], axis=1)
        both = jnp.dot(
            jnp.concatenate([real, imag]), right, preferred_element_type=jnp.float32
        )
        acc[0, to, :] += both[:block]
        acc[1, to, :] += both[block:]

    def update_piece(group, index):
        at_rows, to = block_at(group), block_at(index)
        freal, fimag = gfac[0, at_rows, to].T, gfac[1, at_rows, to].T
        right = terms[pl.ds(pl.multiple_of(2 * group * block, block), 2 * block), :]
        real = jnp.concatenate([freal, -fimag], axis=1)
        imag = jnp.concatenate([fimag, freal], axis=1)
        both = jnp.dot(
            jnp.concatenate([real, imag]), right, preferred_element_type=jnp.float32
        )
        upd[0, to, :] -= both[:block]
        upd[1, to, :] -= both[block:]

    def update_block(index):
        to = block_at(index)
        freal, fimag = gfac[0, :, to].T, gfac[1, :, to].T
        lines = []
        for first, second in ((freal, -fimag), (fimag, freal)):
            pieces = []
            for group in range(blocks):
                cols = slice(group * block, (group + 1) * block)
                pieces += [first[:, cols], second[:, cols]]
            lines.append(jnp.concatenate(pieces, axis=1))
        both = jnp.dot(
            jnp.concatenate(lines),
            terms[pl.ds(0, 2 * panel), :],
            preferred_element_type=jnp.float32,
        )
        upd[0, to, :] -= both[:block]
        upd[1, to, :] -= both[block:]

    stores = (
        pltpu.make_async_copy(acc, solved_ref, local.at[0]),
        pltpu.make_async_copy(upd, updated_ref, local.at[1]),
    )
    last_round = levels + 2 + lag
    solved_at = levels + 3

    def apart(group):
        return jnp.abs(z - group // 2) + jnp.abs(y - lax.rem(group, 2))

    def first_round(group):
        return jnp.maximum(apart(group) + 2 + lag, solved_at)

    def solve_count(group, turn):
        return jnp.where(apart(group) + 2 == turn, blocks - group, 0)

    def update_count(group, turn):
        return jnp.where(jnp.logical_and(turn == last_round, group < tail), 1, 0)

    def run_pieces(turn, first, last):
        def find(number, count):
            def scan(group, carry):
                rest, found = carry
                size = count(group, turn)
                found = jnp.where(jnp.logical_and(found < 0, rest < size), group, found)
                return jnp.where(found < 0, rest - size, rest), found

            return lax.fori_loop(0, blocks, scan, (number, jnp.int32(-1)))

        @pl.when(turn < solved_at)
        def _():
            @pl.loop(first, last)
            def _(number):
                rest, group = find(number, solve_count)
                solve_piece(group, group + rest)

        @pl.when(turn >= solved_at)
        def _():
            @pl.loop(first, last)
            def _(number):
                rest, group = find(number, update_count)
                update_block(group)

    def distance_to(chip):
        zo, yo, xo = chip // 4, lax.rem(chip // 2, 2), lax.rem(chip, 2)
        return jnp.abs(z - zo) + jnp.abs(y - yo) + jnp.abs(x - xo)

    def in_round(chip, turn):
        distance = distance_to(chip)
        first = distance == turn
        second = jnp.logical_and(distance == turn - lag, turn > lag)
        return first, second

    def one_round(turn, carry):
        @pl.when(turn == lag)
        def _():
            send_own(2)
            send_own(3)

        @pl.when(turn == solved_at)
        def _():
            @pl.loop(0, blocks)
            def _(index):
                for part in range(2):
                    to = pl.ds(pl.multiple_of((2 * index + part) * block, block), block)
                    terms[to, :] = acc[part, block_at(index), :].astype(jnp.bfloat16)

            stores[0].start()

        def arrivals(chip, carry):
            other = chip * 2 + 1 - core
            group = chip // 2

            @pl.when(apart(group) + 2 == turn)
            def _():
                arrive_other(0, other)
                arrive_other(1, other)

            @pl.when(first_round(group) == turn)
            def _():
                arrive_other(2, other)
                arrive_other(3, other)

            return carry

        lax.fori_loop(0, chips, arrivals, 0)

        def add_pieces(group, total):
            return total + jnp.where(
                turn < solved_at, solve_count(group, turn), update_count(group, turn)
            )

        def add_events(chip, total):
            first, second = in_round(chip, turn)
            return total + jnp.where(jnp.logical_or(first, second), 1, 0)

        pieces = lax.fori_loop(0, blocks, add_pieces, jnp.int32(0))
        slots = lax.fori_loop(0, chips, add_events, jnp.int32(1))

        def visit(chip, slot):
            zo, yo, xo = chip // 4, lax.rem(chip // 2, 2), lax.rem(chip, 2)
            origin = chip * 2 + core
            first, second = in_round(chip, turn)
            either = jnp.logical_or(first, second)

            for kinds, now in (((0, 1), first), ((2, 3), second)):

                @pl.when(now)
                def _(kinds=kinds):
                    for kind in kinds:
                        goes = onward(kind, zo, yo, xo)

                        def arrive(cls, kind=kind, goes=goes):
                            remote(kind, origin, cls, 4, False).wait_recv()
                            forward(kind, origin, goes, cls, False, "start")

                        by_class(kind, origin, arrive)

            @pl.when(either)
            def _():
                run_pieces(turn, slot * pieces // slots, (slot + 1) * pieces // slots)

            return slot + jnp.where(either, 1, 0)

        lax.fori_loop(0, chips, visit, jnp.int32(0))
        run_pieces(turn, (slots - 1) * pieces // slots, pieces)
        return carry

    lax.fori_loop(1, levels + 3 + lag, one_round, 0)

    stores[1].start()

    def finish(chip, carry):
        zo, yo, xo = chip // 4, lax.rem(chip // 2, 2), lax.rem(chip, 2)
        origin = chip * 2 + core
        for kind in range(4):
            goes = onward(kind, zo, yo, xo)
            by_class(
                kind,
                origin,
                lambda cls, kind=kind, goes=goes: forward(kind, origin, goes, cls, False, "wait"),
            )
        return carry

    lax.fori_loop(0, chips, finish, 0)
    for copy in stores:
        copy.wait()


def fused_body(devices, linv_t, rhs_top, factor_t, rhs_rest):
    parts, rows, panel = linv_t.shape
    trail, width = rhs_rest.shape[1:]
    return pl.pallas_call(
        functools.partial(fused_kernel, devices, LAG),
        out_shape=(
            jax.ShapeDtypeStruct(rhs_top.shape, jnp.float32),
            jax.ShapeDtypeStruct(rhs_rest.shape, jnp.float32),
        ),
        in_specs=[pl.BlockSpec(memory_space=pl.ANY)] * 4,
        out_specs=[pl.BlockSpec(memory_space=pl.ANY)] * 2,
        scratch_shapes=[
            pltpu.VMEM((parts, panel, panel), linv_t.dtype),
            pltpu.VMEM((parts, panel, trail), factor_t.dtype),
            pltpu.VMEM((4 * panel, width), jnp.bfloat16),
            pltpu.VMEM(rhs_top.shape, jnp.float32),
            pltpu.VMEM(rhs_rest.shape, jnp.float32),
            pltpu.SemaphoreType.DMA((4, devices)),
            pltpu.SemaphoreType.DMA((5, 4, devices // 2)),
            pltpu.SemaphoreType.DMA((4,)),
        ],
        compiler_params=pltpu.CompilerParams(
            collective_id=0, has_side_effects=True, vmem_limit_bytes=60 << 20
        ),
    )(linv_t, rhs_top, factor_t, rhs_rest)


def solution(mesh):
    devices = mesh.shape["ang"]
    if mesh.shape["row"] == 1 and devices % 8 == 0:
        body = functools.partial(fused_body, devices)
    else:
        body = general_body
    return jax.shard_map(
        body,
        mesh=mesh,
        in_specs=(
            P(None, "ang", "row"),
            P(None, "row", "ang"),
            P(None, "ang", "row"),
            P(None, "row", "ang"),
        ),
        out_specs=(P(None, "row", "ang"), P(None, "row", "ang")),
        check_vma=False,
    )
```

profile of v0, /device:TPU:29, one launch (start us, length us, event | category | flops | bytes accessed | tf_op | source)
XLA Modules:
  0.0 115.5 jit_solution(17084986994564230112)
XLA Ops:
  0.6 104.9 %shard_map.59 = (f32[2,2048,512]{2,1,0:T(8,128)}, f32[2,1024,512]{2,1,0:T(8,128)}) custom-call(bf16[2,64,2048]{2,1,0:T(8,128)(2,1)} %lin_ref.1, f32[2,2048,512]{2,1,0:T(8,128)} %top_ref.1, bf16[2,64,1024]{2,1,0:T(8,128)(2,1)} %fac_ref.1, f32[2,1024,512]{2,1,0:T(8,128)} %rest_ref.1), custom_call_target="tpu_custom_call" | custom-call | tf_op jit(solution)/shard_map/pallas_call | solution.py:375
  105.6 0.0 copy-start
  105.6 7.9 %copy.8 = f32[2,2048,512]{2,1,0:T(8,128)} copy(f32[2,2048,512]{2,1,0:T(8,128)} %get-tuple-element.4) | data formatting | bytes 16777216
  113.5 0.0 copy-done
  113.5 2.0 %copy.9 = f32[2,1024,512]{2,1,0:T(8,128)} copy(f32[2,1024,512]{2,1,0:T(8,128)S(1)} %copy-done) | data formatting | bytes 8388608
Async XLA Ops:
  105.6 8.0 %copy-start = (f32[2,1024,512]{2,1,0:T(8,128)S(1)}, f32[2,1024,512]{2,1,0:T(8,128)}, u32[]{:S(2)}) copy-start(f32[2,1024,512]{2,1,0:T(8,128)} %get-tuple-element.5) | copy-start | bytes 12582916
where the time goes:
time: 118 us; the launch traced here: 116 us
  Pallas kernels  105 us (89%)
  local copies, waits for them, and re-layouts  9.96 us (8%)
    pallas_call x1, Pallas kernels, fused_body(): pl.pallas_call(functools.partial(fused_kernel, devices, LAG), out_shape=(...  105 us
    unnamed x4, local copies, waits for them, and re-layouts  9.96 us

commit v1 on v0

--- a/solution.py
+++ b/solution.py
@@ -43,8 +43,8 @@
 
 
 def fused_kernel(
-    devices, lag, lin_ref, top_ref, fac_ref, rest_ref, solved_ref, updated_ref,
-    glin, gfac, terms, acc, upd, recv, send, local,
+    devices, lag, lin_ref, top_ref, fac_ref, rest_ref, acc, upd,
+    glin, gfac, terms, recv, send, local,
 ):
     levels = devices // 8
     chips = devices // 2
@@ -220,10 +220,6 @@
         upd[0, to, :] -= both[:block]
         upd[1, to, :] -= both[block:]
 
-    stores = (
-        pltpu.make_async_copy(acc, solved_ref, local.at[0]),
-        pltpu.make_async_copy(upd, updated_ref, local.at[1]),
-    )
     last_round = levels + 2 + lag
     solved_at = levels + 3
 
@@ -287,8 +283,6 @@
                     to = pl.ds(pl.multiple_of((2 * index + part) * block, block), block)
                     terms[to, :] = acc[part, block_at(index), :].astype(jnp.bfloat16)
 
-            stores[0].start()
-
         def arrivals(chip, carry):
             other = chip * 2 + 1 - core
             group = chip // 2
@@ -349,8 +343,6 @@
         return carry
 
     lax.fori_loop(1, levels + 3 + lag, one_round, 0)
-
-    stores[1].start()
 
     def finish(chip, carry):
         zo, yo, xo = chip // 4, lax.rem(chip // 2, 2), lax.rem(chip, 2)
@@ -365,6 +357,15 @@
         return carry
 
     lax.fori_loop(0, chips, finish, 0)
+
+
+def store_kernel(acc, upd, solved_ref, updated_ref, sems):
+    stores = (
+        pltpu.make_async_copy(acc, solved_ref, sems.at[0]),
+        pltpu.make_async_copy(upd, updated_ref, sems.at[1]),
+    )
+    for copy in stores:
+        copy.start()
     for copy in stores:
         copy.wait()
 
@@ -372,28 +373,37 @@
 def fused_body(devices, linv_t, rhs_top, factor_t, rhs_rest):
     parts, rows, panel = linv_t.shape
     trail, width = rhs_rest.shape[1:]
-    return pl.pallas_call(
+    held = pl.pallas_call(
         functools.partial(fused_kernel, devices, LAG),
         out_shape=(
-            jax.ShapeDtypeStruct(rhs_top.shape, jnp.float32),
-            jax.ShapeDtypeStruct(rhs_rest.shape, jnp.float32),
+            pltpu.VMEM(rhs_top.shape, jnp.float32),
+            pltpu.VMEM(rhs_rest.shape, jnp.float32),
         ),
         in_specs=[pl.BlockSpec(memory_space=pl.ANY)] * 4,
-        out_specs=[pl.BlockSpec(memory_space=pl.ANY)] * 2,
+        out_specs=[pl.BlockSpec(memory_space=pltpu.VMEM)] * 2,
         scratch_shapes=[
             pltpu.VMEM((parts, panel, panel), linv_t.dtype),
             pltpu.VMEM((parts, panel, trail), factor_t.dtype),
             pltpu.VMEM((4 * panel, width), jnp.bfloat16),
-            pltpu.VMEM(rhs_top.shape, jnp.float32),
-            pltpu.VMEM(rhs_rest.shape, jnp.float32),
             pltpu.SemaphoreType.DMA((4, devices)),
             pltpu.SemaphoreType.DMA((5, 4, devices // 2)),
             pltpu.SemaphoreType.DMA((4,)),
         ],
         compiler_params=pltpu.CompilerParams(
-            collective_id=0, has_side_effects=True, vmem_limit_bytes=60 << 20
+            collective_id=0, has_side_effects=True, vmem_limit_bytes=48 << 20
         ),
     )(linv_t, rhs_top, factor_t, rhs_rest)
+    return pl.pallas_call(
+        store_kernel,
+        out_shape=(
+            jax.ShapeDtypeStruct(rhs_top.shape, jnp.float32),
+            jax.ShapeDtypeStruct(rhs_rest.shape, jnp.float32),
+        ),
+        in_specs=[pl.BlockSpec(memory_space=pltpu.VMEM)] * 2,
+        out_specs=[pl.BlockSpec(memory_space=pl.ANY)] * 2,
+        scratch_shapes=[pltpu.SemaphoreType.DMA((2,))],
+        compiler_params=pltpu.CompilerParams(vmem_limit_bytes=8 << 20),
+    )(*(pltpu.with_memory_space_constraint(array, pltpu.VMEM) for array in held))
 
 
 def solution(mesh):

time: 118 us -> 113 us (0.958)
  local copies, waits for them, and re-layouts: 9.96 us -> 0 us
  Pallas kernels: 105 us -> 110 us
    unnamed x4 -> x0, local copies, waits for them, and re-layouts: 9.96 us -> none
    pallas_call x0 -> x1, Pallas kernels: none -> 4.79 us  [fused_body(): pl.pallas_call(store_kernel, out_shape=(jax.ShapeDtypeStruct(rhs_top.shap...]
where the time goes in v1:
time: 113 us; the launch traced here: 110 us
  Pallas kernels  110 us (97%)
    pallas_call x1, Pallas kernels, fused_body(): pl.pallas_call(functools.partial(fused_kernel, devices, LAG), out_shape=(...  105 us
    pallas_call x1, Pallas kernels, fused_body(): pl.pallas_call(store_kernel, out_shape=(jax.ShapeDtypeStruct(rhs_top.shap...  4.79 us

profile of v1, /device:TPU:29, one launch (start us, length us, event | category | flops | bytes accessed | tf_op | source)
XLA Modules:
  0.0 110.4 jit_solution(16134111501848732174)
XLA Ops:
  0.6 105.0 %shard_map.59 = (f32[2,2048,512]{2,1,0:T(8,128)S(1)}, f32[2,1024,512]{2,1,0:T(8,128)S(1)}) custom-call(bf16[2,64,2048]{2,1,0:T(8,128)(2,1)} %lin_ref.1, f32[2,2048,512]{2,1,0:T(8,128)} %top_ref.1, bf16[2,64,1024]{2,1,0:T(8,128)(2,1)} %fac_ref.1, f32[2,1024,512]{2,1,0:T(8,128)} %rest_ref.1), custom_call_target="tpu_custom_call" | custom-call | tf_op jit(solution)/shard_map/pallas_call | solution.py:376
  105.6 4.8 %shard_map.60 = (f32[2,2048,512]{2,1,0:T(8,128)}, f32[2,1024,512]{2,1,0:T(8,128)}) custom-call(f32[2,2048,512]{2,1,0:T(8,128)S(1)} %get-tuple-element.4.acc, f32[2,1024,512]{2,1,0:T(8,128)S(1)} %get-tuple-element.5.upd), custom_call_target="tpu_custom_call" | custom-call | tf_op jit(solution)/shard_map/pallas_call | solution.py:396

commit v2 on v1

v2 whole, which is shorter than its diff:
```python
import functools

import jax
import jax.numpy as jnp
from jax import lax
from jax.experimental import pallas as pl
from jax.experimental.pallas import tpu as pltpu
from jax.sharding import PartitionSpec as P

DIMS0 = (((0,), (0,)), ((), ()))
LEVELS = 4
PLAN = (
    (
        516, 513, 514, 148, 8, 145, 146, 132888, 1541, 132614, 1576, 1174,
        1173, 1539, 34826, 2616, 34825, 34956, 68508, 34963, 35874, 69402, 35873, 3890,
        3865, 135596, 4516, 4913, 102542, 4148, 4615, 4650, 4649, 4247, 4924, 4666,
        104349, 6046, 70667, 5689, 5261, 5915, 5550, 5939, 105901, 7222, 7203, 40079,
        40765, 8095, 7221, 7723, 46910, 177583, 111671, 13883, 145830, 14757, 115519, 17831,
    ),
    (
        8, 517, 518, 792, 512, 149, 150, 552, 33801, 33802, 1168, 34360,
        33932, 34716, 34311, 1537, 1817, 100780, 2190, 2194, 35610, 2601, 2199, 2080,
        2562, 2876, 2973, 69534, 3888, 101930, 3642, 3502, 3217, 3083, 3501, 102969,
        4237, 4925, 6047, 5635, 203547, 6961, 6575, 6566, 6287, 109715, 11685, 142390,
        11317, 45611, 77858, 46113, 243518, 14130, 144807, 47159, 81467, 48163, 148287, 18227,
    ),
    (
        140, 924, 9, 10, 516, 793, 794, 428, 33934, 1172, 1577, 1578,
        1852, 1949, 1593, 34362, 1950, 34957, 35328, 34827, 2566, 35246, 2477, 2198,
        2843, 2565, 2191, 102205, 3999, 3627, 4240, 4245, 71486, 71087, 71227, 5633,
        38034, 5540, 5634, 5172, 5271, 5639, 5152, 39743, 72849, 139056, 40083, 79363,
        13365, 46897, 46134, 144806, 13733, 13345, 48162, 114482, 80951, 212787, 114723, 17831,
    ),
    (
        141, 142, 1949, 1950, 66568, 1816, 1454, 1453, 1167, 1576, 1854, 1853,
        1951, 1592, 34826, 2057, 2842, 2564, 2479, 2841, 2601, 2602, 69439, 3220,
        69177, 3083, 3642, 3584, 3589, 3590, 3222, 3867, 3221, 169515, 5264, 38459,
        103937, 5271, 5634, 5266, 5540, 5639, 5172, 171153, 39968, 40451, 144531, 13365,
        14128, 111670, 13346, 14129, 13345, 145830, 15154, 14391, 245157, 16179, 114723, 17831,
    ),
)
ORDER = (
    (
        0, 2, 1, 4, 3, 6, 5, 7, 0, 4, 1, 6,
        5, 2, 7, 3,
    ),
    (
        2, 4, 3, 0, 6, 5, 7, 1, 4, 6, 2, 0,
        3, 5, 7, 1,
    ),
    (
        4, 6, 5, 7, 2, 3, 0, 1, 4, 6, 5, 7,
        2, 0, 1, 3,
    ),
    (
        6, 7, 4, 5, 2, 3, 0, 1, 6, 7, 4, 5,
        0, 2, 1, 3,
    ),
)
OWN_AT = (8, 20, 0, 1)
L_CUTS, F_CUTS, TOP_CUTS = 1, 1, 1
DRAIN = 30
LEFT = 17


def tdot(first, second):
    return lax.dot_general(first, second, DIMS0, preferred_element_type=jnp.float32)


def split_two(value):
    high = value.astype(jnp.bfloat16)
    low = (value - high.astype(jnp.float32)).astype(jnp.bfloat16)
    return high, low


def general_body(linv_t, rhs_top, factor_t, rhs_rest):
    top_all = lax.all_gather(rhs_top, "row", axis=1, tiled=True)
    high, low = split_two(top_all)
    inverse = lax.all_gather(linv_t, "ang", axis=1, tiled=True)

    def single(first, second):
        return tdot(inverse[first], high[second]) + tdot(inverse[first], low[second])

    solved = jnp.stack([single(0, 0) - single(1, 1), single(0, 1) + single(1, 0)])
    half = lax.all_gather(solved.astype(jnp.bfloat16), "row", axis=1, tiled=True)
    factor = lax.all_gather(factor_t, "ang", axis=1, tiled=True)
    update = jnp.stack(
        [
            tdot(factor[0], half[0]) - tdot(factor[1], half[1]),
            tdot(factor[0], half[1]) + tdot(factor[1], half[0]),
        ]
    )
    return (solved, rhs_rest - update)


def fused_kernel(
    lin_ref, top_ref, fac_ref, rest_ref, acc, upd,
    glin, gfac, terms, recv, send, local,
):
    rows = lin_ref.shape[1]
    panel = lin_ref.shape[2]
    width = top_ref.shape[2]
    lane = 2 * rows
    block = 4 * rows
    blocks = panel // block
    chips = panel // lane
    wide = 2 * block
    tail = fac_ref.shape[2] // wide
    events = len(PLAN[0])
    l_kinds, f_kinds = 2 * L_CUTS, 2 * F_CUTS
    l_rows, f_rows = rows // L_CUTS, rows // F_CUTS

    me = lax.axis_index("ang")
    core = lax.rem(me, 2)
    x = lax.rem(me // 2, 2)
    y = lax.rem(me // 4, 2)
    z = me // 8
    chip = me // 2
    has_up, has_down = z < LEVELS - 1, z > 0
    targets = (
        me + 2 - 4 * x,
        me + 4 - 8 * y,
        jnp.where(has_up, me + 8, me),
        jnp.where(has_down, me - 8, me),
        me + 1 - 2 * core,
    )
    mine = pl.ds(pl.multiple_of(me * rows, rows), rows)

    def at_level(values):
        result = jnp.int32(values[0])
        for level in range(1, LEVELS):
            result = jnp.where(z == level, jnp.int32(values[level]), result)
        return result

    plan = [at_level([PLAN[level][index] for level in range(LEVELS)]) for index in range(events)]
    order = [
        at_level([ORDER[level][index] for level in range(LEVELS)]) for index in range(2 * blocks)
    ]

    def pick(words, index):
        result = words[0]
        for place in range(1, len(words)):
            result = jnp.where(index == place, words[place], result)
        return result

    own_at = at_level(OWN_AT)

    top_rows = panel // TOP_CUTS
    top_loads = [
        pltpu.make_async_copy(
            top_ref.at[:, pl.ds(cut * top_rows, top_rows), :],
            acc.at[:, pl.ds(cut * top_rows, top_rows), :],
            local.at[cut],
        )
        for cut in range(TOP_CUTS)
    ]
    loads = (
        pltpu.make_async_copy(lin_ref, glin.at[:, mine, :], local.at[TOP_CUTS]),
        pltpu.make_async_copy(fac_ref, gfac.at[:, mine, :], local.at[TOP_CUTS + 1]),
        pltpu.make_async_copy(rest_ref, upd, local.at[TOP_CUTS + 2]),
    )
    for copy in (*top_loads, *loads):
        copy.start()

    barrier = pltpu.get_barrier_semaphore()

    def greet(target):
        pl.semaphore_signal(
            barrier, inc=1, device_id={"ang": target}, device_id_type=pl.DeviceIdType.MESH
        )

    for index in (0, 1, 4):
        greet(targets[index])
    pl.when(has_up)(lambda: greet(targets[2]))
    pl.when(has_down)(lambda: greet(targets[3]))
    pl.semaphore_wait(barrier, 3 + has_up.astype(jnp.int32) + has_down.astype(jnp.int32))

    def block_at(index):
        return pl.ds(pl.multiple_of(index * block, block), block)

    def by_class(origin_chip, action):
        for quad in range(chips // 4):

            @pl.when(origin_chip // 4 == quad)
            def _(quad=quad):
                for cls in range(4 * quad, 4 * quad + 4):
                    pl.when(origin_chip == cls)(functools.partial(action, cls))

    def l_place(kind, origin, cls):
        at = pl.multiple_of(origin * rows + (kind // 2) * l_rows, l_rows)
        return glin.at[lax.rem(kind, 2), pl.ds(at, l_rows), pl.ds(cls * lane, panel - cls * lane)]

    def l_source(kind, cls):
        at = (kind // 2) * l_rows
        return lin_ref.at[kind % 2, pl.ds(at, l_rows), pl.ds(cls * lane, panel - cls * lane)]

    def f_place(kind, origin):
        at = pl.multiple_of(origin * rows + (kind // 2) * f_rows, f_rows)
        return gfac.at[lax.rem(kind, 2), pl.ds(at, f_rows), :]

    def f_source(kind):
        return fac_ref.at[kind % 2, pl.ds((kind // 2) * f_rows, f_rows), :]

    def remote(source, place, slot, origin, direction):
        return pltpu.make_async_remote_copy(
            src_ref=source,
            dst_ref=place,
            send_sem=send.at[direction, slot, origin // 2],
            recv_sem=recv.at[slot, origin],
            device_id={"ang": targets[direction]},
            device_id_type=pl.DeviceIdType.MESH,
        )

    def l_copy(kind, origin, cls, direction, own):
        source = l_source(kind, cls) if own else l_place(kind, origin, cls)
        return remote(source, l_place(jnp.int32(kind), origin, cls), kind, origin, direction)

    def f_copy(kind, origin, direction, own):
        source = f_source(kind) if own else f_place(kind, origin)
        return remote(source, f_place(jnp.int32(kind), origin), l_kinds + kind, origin, direction)

    def spread(copy_of, goes, act):
        for direction in range(5):
            copy = copy_of(direction)
            run = copy.start if act == "start" else copy.wait_send
            if goes[direction] is True:
                run()
            else:
                pl.when(goes[direction])(run)

    own_goes = (True, True, has_up, has_down, True)

    def own_l(act):
        def run(cls):
            for kind in range(l_kinds):
                spread(lambda way, kind=kind: l_copy(kind, me, cls, way, True), own_goes, act)

        by_class(chip, run)

    def own_f(act):
        for kind in range(f_kinds):
            spread(lambda way, kind=kind: f_copy(kind, me, way, True), own_goes, act)

    own_l("start")

    def split_piece(index):
        at_rows = block_at(index)
        for part in range(2):
            first, second = split_two(acc[part, at_rows, :])
            terms[pl.ds(pl.multiple_of((4 * index + 2 * part) * block, block), block), :] = first
            terms[pl.ds(pl.multiple_of((4 * index + 2 * part + 1) * block, block), block), :] = second
            acc[part, at_rows, :] = jnp.zeros((block, width), jnp.float32)

    for cut in range(TOP_CUTS):
        top_loads[cut].wait()

        @pl.loop(cut * blocks // TOP_CUTS, (cut + 1) * blocks // TOP_CUTS)
        def _(index):
            split_piece(index)

    for copy in loads:
        copy.wait()

    for index in range(blocks):
        for part in range(2):
            glin[
                part, pl.ds(index * block + lane, lane), pl.ds(index * block, lane)
            ] = jnp.zeros((lane, lane), glin.dtype)

    def solve_piece(group, index):
        at_rows, to = block_at(group), block_at(index)
        lreal, limag = glin[0, at_rows, to].T, glin[1, at_rows, to].T
        right = terms[pl.ds(pl.multiple_of(4 * group * block, block), 4 * block), :]
        real = jnp.concatenate([lreal, lreal, -limag, -limag], axis=1)
        imag = jnp.concatenate([limag, limag, lreal, lreal], axis=1)
        both = jnp.dot(
            jnp.concatenate([real, imag]), right, preferred_element_type=jnp.float32
        )
        acc[0, to, :] += both[:block]
        acc[1, to, :] += both[block:]

    def half_piece(index):
        at_rows = block_at(index)
        real = acc[0, at_rows, :].astype(jnp.bfloat16)
        imag = acc[1, at_rows, :].astype(jnp.bfloat16)
        for place, value in enumerate((-imag, real, imag)):
            to = pl.ds(pl.multiple_of((3 * index + place) * block, block), block)
            terms[to, :] = value

    def update_piece(group, index):
        at_rows, to = block_at(group), pl.ds(pl.multiple_of(index * wide, wide), wide)
        left = jnp.concatenate([gfac[1, at_rows, to].T, gfac[0, at_rows, to].T], axis=1)
        for part in range(2):
            right = terms[
                pl.ds(pl.multiple_of((3 * group + part) * block, block), 2 * block), :
            ]
            upd[part, to, :] -= jnp.dot(left, right, preferred_element_type=jnp.float32)

    def arrive_l(group):
        for side in range(2):
            origin_chip = 2 * group + side
            other = 2 * origin_chip + 1 - core

            def run(cls, other=other):
                for kind in range(l_kinds):
                    l_copy(kind, other, cls, 4, False).wait_recv()

            by_class(origin_chip, run)

    def arrive_f(group):
        for side in range(2):
            other = 2 * (2 * group + side) + 1 - core
            for kind in range(f_kinds):
                f_copy(kind, other, 4, False).wait_recv()

    def step(limit, state):
        slot, index = state
        active = slot < limit
        is_half = slot == blocks
        relative = pick(order, jnp.where(slot > blocks, slot - 1, slot))
        group = 2 * (relative // 2) + lax.rem(y + lax.rem(relative, 2), 2)

        @pl.when(jnp.logical_and(active, slot < blocks))
        def _():
            pl.when(index == 0)(lambda: arrive_l(group))
            solve_piece(group, group + index)

        @pl.when(jnp.logical_and(active, is_half))
        def _():
            half_piece(index)

        @pl.when(jnp.logical_and(active, slot > blocks))
        def _():
            pl.when(index == 0)(lambda: arrive_f(group))
            update_piece(group, index)

        size = jnp.where(slot < blocks, blocks - group, jnp.where(is_half, blocks, tail))
        done = index + 1 >= size
        next_slot = jnp.where(done, slot + 1, slot)
        next_index = jnp.where(done, 0, index + 1)
        return jnp.where(active, next_slot, slot), jnp.where(active, next_index, index)

    def decode(event):
        field = pick(plan, event)
        code = lax.rem(field, 128)
        way = lax.rem(field // 128, 8)
        kind, zo, near = code // 16, lax.rem(code // 4, 4), lax.rem(code, 4)
        xo = lax.rem(x + lax.rem(near, 2), 2)
        yo = lax.rem(y + near // 2, 2)
        same_x, same_y, same_z = lax.rem(near, 2) == 0, near // 2 == 0, z == zo
        x_first_y, x_first_z, y_first_z = way // 4 == 1, lax.rem(way // 2, 2) == 1, lax.rem(way, 2) == 1

        def implied(first, second):
            return jnp.logical_or(jnp.logical_not(first), second)

        free_x = jnp.logical_and(implied(x_first_y, same_y), implied(x_first_z, same_z))
        free_y = jnp.logical_and(jnp.logical_or(x_first_y, same_x), implied(y_first_z, same_z))
        free_z = jnp.logical_and(jnp.logical_or(x_first_z, same_x), jnp.logical_or(y_first_z, same_y))
        goes = (
            jnp.logical_and(free_x, same_x),
            jnp.logical_and(free_y, same_y),
            jnp.logical_and(free_z, jnp.logical_and(z >= zo, has_up)),
            jnp.logical_and(free_z, jnp.logical_and(z <= zo, has_down)),
            True,
        )
        origin_chip = 4 * zo + 2 * yo + xo
        return kind, origin_chip, goes, lax.rem(field // 1024, 32), field // 32768

    def run_event(event, act):
        kind, origin_chip, goes, ready, steps = decode(event)
        origin = 2 * origin_chip + core

        @pl.when(kind < l_kinds)
        def _():
            def run(cls):
                if act == "start":
                    l_copy(kind, origin, cls, 4, False).wait_recv()
                spread(lambda way: l_copy(kind, origin, cls, way, False), goes, act)

            by_class(origin_chip, run)

        @pl.when(kind >= l_kinds)
        def _():
            if act == "start":
                f_copy(kind - l_kinds, origin, 4, False).wait_recv()
            spread(lambda way: f_copy(kind - l_kinds, origin, way, False), goes, act)

        return ready, steps

    def one_event(event, state):
        pl.when(event == own_at)(lambda: own_f("start"))
        ready, steps = run_event(event, "start")

        @pl.when(event >= DRAIN)
        def _():
            run_event(event - DRAIN, "wait")

        return lax.fori_loop(0, steps, lambda _, now: step(ready, now), state)

    state = lax.fori_loop(0, events, one_event, (jnp.int32(0), jnp.int32(0)))
    slots = 2 * blocks + 1
    pieces = blocks * (blocks + 1) // 2 + blocks + blocks * tail
    lax.fori_loop(0, LEFT, lambda _, now: step(slots, now), state)

    @pl.loop(events - DRAIN, events)
    def _(event):
        run_event(event, "wait")

    own_l("wait")
    own_f("wait")


def store_kernel(acc, upd, solved_ref, updated_ref, sems):
    stores = (
        pltpu.make_async_copy(acc, solved_ref, sems.at[0]),
        pltpu.make_async_copy(upd, updated_ref, sems.at[1]),
    )
    for copy in stores:
        copy.start()
    for copy in stores:
        copy.wait()


def fused_body(devices, linv_t, rhs_top, factor_t, rhs_rest):
    parts, _, panel = linv_t.shape
    trail = rhs_rest.shape[1]
    width = rhs_top.shape[2]
    kinds = 2 * (L_CUTS + F_CUTS)
    held = pl.pallas_call(
        fused_kernel,
        out_shape=(
            pltpu.VMEM(rhs_top.shape, jnp.float32),
            pltpu.VMEM(rhs_rest.shape, jnp.float32),
        ),
        in_specs=[pl.BlockSpec(memory_space=pl.ANY)] * 4,
        out_specs=[pl.BlockSpec(memory_space=pltpu.VMEM)] * 2,
        scratch_shapes=[
            pltpu.VMEM((parts, panel, panel), linv_t.dtype),
            pltpu.VMEM((parts, panel, trail), factor_t.dtype),
            pltpu.VMEM((4 * panel, width), jnp.bfloat16),
            pltpu.SemaphoreType.DMA((kinds, devices)),
            pltpu.SemaphoreType.DMA((5, kinds, devices // 2)),
            pltpu.SemaphoreType.DMA((TOP_CUTS + 3,)),
        ],
        compiler_params=pltpu.CompilerParams(
            collective_id=0, has_side_effects=True, vmem_limit_bytes=48 << 20
        ),
    )(linv_t, rhs_top, factor_t, rhs_rest)
    return pl.pallas_call(
        store_kernel,
        out_shape=(
            jax.ShapeDtypeStruct(rhs_top.shape, jnp.float32),
            jax.ShapeDtypeStruct(rhs_rest.shape, jnp.float32),
        ),
        in_specs=[pl.BlockSpec(memory_space=pltpu.VMEM)] * 2,
        out_specs=[pl.BlockSpec(memory_space=pl.ANY)] * 2,
        scratch_shapes=[pltpu.SemaphoreType.DMA((2,))],
        compiler_params=pltpu.CompilerParams(vmem_limit_bytes=8 << 20),
    )(*(pltpu.with_memory_space_constraint(array, pltpu.VMEM) for array in held))


def solution(mesh):
    devices = mesh.shape["ang"]
    if mesh.shape["row"] == 1 and devices == 8 * LEVELS:
        body = functools.partial(fused_body, devices)
    else:
        body = general_body
    return jax.shard_map(
        body,
        mesh=mesh,
        in_specs=(
            P(None, "ang", "row"),
            P(None, "row", "ang"),
            P(None, "ang", "row"),
            P(None, "row", "ang"),
        ),
        out_specs=(P(None, "row", "ang"), P(None, "row", "ang")),
        check_vma=False,
    )
```

time: 113 us -> 102 us (0.903); the launches traced: 110 us -> 101 us
  Pallas kernels: 110 us -> 101 us
    pallas_call x1, Pallas kernels: 105 us -> 96 us  [fused_body(): pl.pallas_call(fused_kernel, out_shape=(pltpu.VMEM(rhs_top.shape, jnp.flo...]
where the time goes in v2:
time: 102 us; the launch traced here: 101 us
  Pallas kernels  101 us (99%)
    pallas_call x1, Pallas kernels, fused_body(): pl.pallas_call(fused_kernel, out_shape=(pltpu.VMEM(rhs_top.shape, jnp.flo...  96 us
    pallas_call x1, Pallas kernels, fused_body(): pl.pallas_call(store_kernel, out_shape=(jax.ShapeDtypeStruct(rhs_top.shap...  4.79 us

profile of v2, /device:TPU:29, one launch (start us, length us, event | category | flops | bytes accessed | tf_op | source)
XLA Modules:
  0.0 101.5 jit_solution(2168683593757830302)
XLA Ops:
  0.6 96.0 %shard_map.59 = (f32[2,2048,512]{2,1,0:T(8,128)S(1)}, f32[2,1024,512]{2,1,0:T(8,128)S(1)}) custom-call(bf16[2,64,2048]{2,1,0:T(8,128)(2,1)} %lin_ref.1, f32[2,2048,512]{2,1,0:T(8,128)} %top_ref.1, bf16[2,64,1024]{2,1,0:T(8,128)(2,1)} %fac_ref.1, f32[2,1024,512]{2,1,0:T(8,128)} %rest_ref.1), custom_call_target="tpu_custom_call" | custom-call | tf_op jit(solution)/shard_map/pallas_call | solution.py:429
  96.7 4.8 %shard_map.60 = (f32[2,2048,512]{2,1,0:T(8,128)}, f32[2,1024,512]{2,1,0:T(8,128)}) custom-call(f32[2,2048,512]{2,1,0:T(8,128)S(1)} %get-tuple-element.4.acc, f32[2,1024,512]{2,1,0:T(8,128)S(1)} %get-tuple-element.5.upd), custom_call_target="tpu_custom_call" | custom-call | tf_op jit(solution)/shard_map/pallas_call | solution.py:449

commit v3 on v2

--- a/solution.py
+++ b/solution.py
@@ -11,56 +11,58 @@
 LEVELS = 4
 PLAN = (
     (
-        516, 513, 514, 148, 8, 145, 146, 132888, 1541, 132614, 1576, 1174,
-        1173, 1539, 34826, 2616, 34825, 34956, 68508, 34963, 35874, 69402, 35873, 3890,
-        3865, 135596, 4516, 4913, 102542, 4148, 4615, 4650, 4649, 4247, 4924, 4666,
-        104349, 6046, 70667, 5689, 5261, 5915, 5550, 5939, 105901, 7222, 7203, 40079,
-        40765, 8095, 7221, 7723, 46910, 177583, 111671, 13883, 145830, 14757, 115519, 17831,
-    ),
-    (
-        8, 517, 518, 792, 512, 149, 150, 552, 33801, 33802, 1168, 34360,
-        33932, 34716, 34311, 1537, 1817, 100780, 2190, 2194, 35610, 2601, 2199, 2080,
-        2562, 2876, 2973, 69534, 3888, 101930, 3642, 3502, 3217, 3083, 3501, 102969,
-        4237, 4925, 6047, 5635, 203547, 6961, 6575, 6566, 6287, 109715, 11685, 142390,
-        11317, 45611, 77858, 46113, 243518, 14130, 144807, 47159, 81467, 48163, 148287, 18227,
-    ),
-    (
-        140, 924, 9, 10, 516, 793, 794, 428, 33934, 1172, 1577, 1578,
-        1852, 1949, 1593, 34362, 1950, 34957, 35328, 34827, 2566, 35246, 2477, 2198,
-        2843, 2565, 2191, 102205, 3999, 3627, 4240, 4245, 71486, 71087, 71227, 5633,
-        38034, 5540, 5634, 5172, 5271, 5639, 5152, 39743, 72849, 139056, 40083, 79363,
-        13365, 46897, 46134, 144806, 13733, 13345, 48162, 114482, 80951, 212787, 114723, 17831,
-    ),
-    (
-        141, 142, 1949, 1950, 66568, 1816, 1454, 1453, 1167, 1576, 1854, 1853,
-        1951, 1592, 34826, 2057, 2842, 2564, 2479, 2841, 2601, 2602, 69439, 3220,
-        69177, 3083, 3642, 3584, 3589, 3590, 3222, 3867, 3221, 169515, 5264, 38459,
-        103937, 5271, 5634, 5266, 5540, 5639, 5172, 171153, 39968, 40451, 144531, 13365,
-        14128, 111670, 13346, 14129, 13345, 145830, 15154, 14391, 245157, 16179, 114723, 17831,
+        516, 129, 130, 532, 776, 529, 530, 66712, 1420, 1541, 1542, 66588,
+        1801, 1558, 1155, 1422, 1421, 1178, 1964, 1802, 1557, 1555, 68668, 3105,
+        3106, 69785, 4273, 4495, 4274, 5038, 36893, 38820, 38043, 5150, 5639, 38452,
+        38667, 7085, 6179, 38973, 6679, 40879, 7347, 39967, 12350, 45608, 45621, 12854,
+        242232, 12841, 13222, 12842, 12351, 179109, 14905, 48695, 15930, 81831, 48683, 15931,
+    ),
+    (
+        776, 517, 518, 152, 128, 396, 28, 533, 534, 34569, 1802, 1552,
+        67737, 2446, 2445, 2202, 35335, 34945, 2988, 2077, 2178, 2078, 2108, 3104,
+        36375, 37643, 4625, 4272, 38287, 6062, 38043, 6674, 72621, 7087, 39043, 6175,
+        39998, 7202, 73256, 7201, 7229, 40504, 7346, 7699, 7345, 77734, 44965, 44598,
+        77365, 242218, 78394, 12841, 12323, 13223, 12351, 12855, 114233, 15915, 15539, 15931,
+    ),
+    (
+        396, 28, 777, 778, 516, 153, 154, 397, 1422, 1053, 67614, 2988,
+        2580, 35595, 2108, 2565, 2203, 2566, 2447, 2176, 4014, 35871, 4630, 37397,
+        6061, 38416, 37949, 6063, 37950, 5639, 38018, 5249, 5152, 5655, 71856, 6674,
+        6673, 7076, 39999, 40490, 40500, 7738, 73257, 7202, 7737, 7346, 7299, 8102,
+        7699, 13221, 12321, 45622, 45233, 46635, 46645, 80443, 244771, 49063, 15927, 15539,
+    ),
+    (
+        397, 398, 29, 30, 776, 33944, 1423, 1966, 1965, 1801, 1086, 1055,
+        1085, 1802, 1540, 1178, 34969, 69551, 3851, 3135, 3604, 3589, 3590, 3227,
+        3200, 70166, 4629, 4624, 4615, 5249, 71208, 5655, 105016, 6674, 6673, 72834,
+        7722, 7721, 39968, 7737, 7738, 72880, 7299, 8100, 7699, 7732, 77857, 45611,
+        45233, 13346, 13490, 243622, 46651, 14245, 81461, 15395, 81462, 15539, 15927, 16295,
     ),
 )
 ORDER = (
     (
-        0, 2, 1, 4, 3, 6, 5, 7, 0, 4, 1, 6,
-        5, 2, 7, 3,
-    ),
-    (
-        2, 4, 3, 0, 6, 5, 7, 1, 4, 6, 2, 0,
-        3, 5, 7, 1,
-    ),
-    (
-        4, 6, 5, 7, 2, 3, 0, 1, 4, 6, 5, 7,
-        2, 0, 1, 3,
-    ),
-    (
-        6, 7, 4, 5, 2, 3, 0, 1, 6, 7, 4, 5,
-        0, 2, 1, 3,
+        0, 2, 1, 4, 6, 5, 3, 7, 0, 6, 1, 7,
+        2, 4, 3, 5,
+    ),
+    (
+        2, 4, 6, 3, 0, 5, 7, 1, 6, 0, 2, 7,
+        3, 4, 1, 5,
+    ),
+    (
+        4, 6, 5, 7, 2, 3, 0, 1, 6, 7, 4, 0,
+        2, 5, 3, 1,
+    ),
+    (
+        6, 7, 4, 5, 2, 3, 0, 1, 6, 7, 4, 0,
+        5, 2, 1, 3,
     ),
 )
-OWN_AT = (8, 20, 0, 1)
+OWN_AT = (8, 30, 30, 2)
 L_CUTS, F_CUTS, TOP_CUTS = 1, 1, 1
 DRAIN = 30
-LEFT = 17
+LEFT = 4
+LATE = 2
+STORE_CUTS = 2
 
 
 def tdot(first, second):
@@ -93,9 +95,28 @@
     return (solved, rhs_rest - update)
 
 
+def group_of(relative, y):
+    return 2 * (relative // 2) + lax.rem(y + lax.rem(relative, 2), 2)
+
+
+def update_piece(gfac, terms, upd, groups, block, start, size):
+    to = pl.ds(start, size)
+    lefts, rights = [], [[], []]
+    for group in groups:
+        at_rows = pl.ds(pl.multiple_of(group * block, block), block)
+        lefts += [gfac[1, at_rows, to].T, gfac[0, at_rows, to].T]
+        for part in range(2):
+            at_terms = pl.ds(pl.multiple_of((3 * group + part) * block, block), 2 * block)
+            rights[part].append(terms[at_terms, :])
+    left = jnp.concatenate(lefts, axis=1)
+    for part in range(2):
+        right = jnp.concatenate(rights[part])
+        upd[part, to, :] -= jnp.dot(left, right, preferred_element_type=jnp.float32)
+
+
 def fused_kernel(
-    lin_ref, top_ref, fac_ref, rest_ref, acc, upd,
-    glin, gfac, terms, recv, send, local,
+    lin_ref, top_ref, fac_ref, rest_ref, acc, upd, gfac, terms,
+    glin, recv, send, local,
 ):
     rows = lin_ref.shape[1]
     panel = lin_ref.shape[2]
@@ -104,8 +125,6 @@
     block = 4 * rows
     blocks = panel // block
     chips = panel // lane
-    wide = 2 * block
-    tail = fac_ref.shape[2] // wide
     events = len(PLAN[0])
     l_kinds, f_kinds = 2 * L_CUTS, 2 * F_CUTS
     l_rows, f_rows = rows // L_CUTS, rows // F_CUTS
@@ -267,8 +286,9 @@
                 part, pl.ds(index * block + lane, lane), pl.ds(index * block, lane)
             ] = jnp.zeros((lane, lane), glin.dtype)
 
-    def solve_piece(group, index):
-        at_rows, to = block_at(group), block_at(index)
+    def solve_piece(group, index, count):
+        size = count * block
+        at_rows, to = block_at(group), pl.ds(pl.multiple_of(index * block, block), size)
         lreal, limag = glin[0, at_rows, to].T, glin[1, at_rows, to].T
         right = terms[pl.ds(pl.multiple_of(4 * group * block, block), 4 * block), :]
         real = jnp.concatenate([lreal, lreal, -limag, -limag], axis=1)
@@ -276,8 +296,8 @@
         both = jnp.dot(
             jnp.concatenate([real, imag]), right, preferred_element_type=jnp.float32
         )
-        acc[0, to, :] += both[:block]
-        acc[1, to, :] += both[block:]
+        acc[0, to, :] += both[:size]
+        acc[1, to, :] += both[size:]
 
     def half_piece(index):
         at_rows = block_at(index)
@@ -287,15 +307,6 @@
             to = pl.ds(pl.multiple_of((3 * index + place) * block, block), block)
             terms[to, :] = value
 
-    def update_piece(group, index):
-        at_rows, to = block_at(group), pl.ds(pl.multiple_of(index * wide, wide), wide)
-        left = jnp.concatenate([gfac[1, at_rows, to].T, gfac[0, at_rows, to].T], axis=1)
-        for part in range(2):
-            right = terms[
-                pl.ds(pl.multiple_of((3 * group + part) * block, block), 2 * block), :
-            ]
-            upd[part, to, :] -= jnp.dot(left, right, preferred_element_type=jnp.float32)
-
     def arrive_l(group):
         for side in range(2):
             origin_chip = 2 * group + side
@@ -318,12 +329,14 @@
         active = slot < limit
         is_half = slot == blocks
         relative = pick(order, jnp.where(slot > blocks, slot - 1, slot))
-        group = 2 * (relative // 2) + lax.rem(y + lax.rem(relative, 2), 2)
+        group = group_of(relative, y)
 
         @pl.when(jnp.logical_and(active, slot < blocks))
         def _():
             pl.when(index == 0)(lambda: arrive_l(group))
-            solve_piece(group, group + index)
+            first = group + 2 * index
+            pl.when(first + 1 < blocks)(lambda: solve_piece(group, first, 2))
+            pl.when(first + 1 == blocks)(lambda: solve_piece(group, first, 1))
 
         @pl.when(jnp.logical_and(active, is_half))
         def _():
@@ -331,10 +344,10 @@
 
         @pl.when(jnp.logical_and(active, slot > blocks))
         def _():
-            pl.when(index == 0)(lambda: arrive_f(group))
-            update_piece(group, index)
-
-        size = jnp.where(slot < blocks, blocks - group, jnp.where(is_half, blocks, tail))
+            arrive_f(group)
+            update_piece(gfac, terms, upd, (group,), block, 0, fac_ref.shape[2])
+
+        size = jnp.where(slot < blocks, (blocks - group + 1) // 2, jnp.where(is_half, blocks, 1))
         done = index + 1 >= size
         next_slot = jnp.where(done, slot + 1, slot)
         next_index = jnp.where(done, 0, index + 1)
@@ -398,25 +411,44 @@
         return lax.fori_loop(0, steps, lambda _, now: step(ready, now), state)
 
     state = lax.fori_loop(0, events, one_event, (jnp.int32(0), jnp.int32(0)))
-    slots = 2 * blocks + 1
-    pieces = blocks * (blocks + 1) // 2 + blocks + blocks * tail
+    slots = 2 * blocks + 1 - LATE
     lax.fori_loop(0, LEFT, lambda _, now: step(slots, now), state)
 
     @pl.loop(events - DRAIN, events)
     def _(event):
         run_event(event, "wait")
 
+    for place in range(2 * blocks - LATE, 2 * blocks):
+        arrive_f(group_of(order[place], y))
     own_l("wait")
     own_f("wait")
 
 
-def store_kernel(acc, upd, solved_ref, updated_ref, sems):
-    stores = (
-        pltpu.make_async_copy(acc, solved_ref, sems.at[0]),
-        pltpu.make_async_copy(upd, updated_ref, sems.at[1]),
-    )
-    for copy in stores:
-        copy.start()
+def store_kernel(acc, upd, gfac, terms, solved_ref, updated_ref, rest, sems):
+    me = lax.axis_index("ang")
+    y = lax.rem(me // 4, 2)
+    z = me // 8
+    trail = gfac.shape[2]
+    block = gfac.shape[1] // (len(ORDER[0]) // 2)
+    size = trail // STORE_CUTS
+    groups = []
+    for place in range(len(ORDER[0]) - LATE, len(ORDER[0])):
+        relative = jnp.int32(ORDER[0][place])
+        for level in range(1, LEVELS):
+            relative = jnp.where(z == level, jnp.int32(ORDER[level][place]), relative)
+        groups.append(group_of(relative, y))
+    stores = [pltpu.make_async_copy(acc, solved_ref, sems.at[0])]
+    stores[0].start()
+    for cut in range(STORE_CUTS):
+        at = pl.ds(cut * size, size)
+        rest[:, at, :] = upd[:, at, :]
+        update_piece(gfac, terms, rest, groups, block, cut * size, size)
+        stores.append(
+            pltpu.make_async_copy(
+                rest.at[:, at, :], updated_ref.at[:, at, :], sems.at[1 + cut]
+            )
+        )
+        stores[-1].start()
     for copy in stores:
         copy.wait()
 
@@ -431,19 +463,19 @@
         out_shape=(
             pltpu.VMEM(rhs_top.shape, jnp.float32),
             pltpu.VMEM(rhs_rest.shape, jnp.float32),
+            pltpu.VMEM((parts, panel, trail), factor_t.dtype),
+            pltpu.VMEM((4 * panel, width), jnp.bfloat16),
         ),
         in_specs=[pl.BlockSpec(memory_space=pl.ANY)] * 4,
-        out_specs=[pl.BlockSpec(memory_space=pltpu.VMEM)] * 2,
+        out_specs=[pl.BlockSpec(memory_space=pltpu.VMEM)] * 4,
         scratch_shapes=[
             pltpu.VMEM((parts, panel, panel), linv_t.dtype),
-            pltpu.VMEM((parts, panel, trail), factor_t.dtype),
-            pltpu.VMEM((4 * panel, width), jnp.bfloat16),
             pltpu.SemaphoreType.DMA((kinds, devices)),
             pltpu.SemaphoreType.DMA((5, kinds, devices // 2)),
             pltpu.SemaphoreType.DMA((TOP_CUTS + 3,)),
         ],
         compiler_params=pltpu.CompilerParams(
-            collective_id=0, has_side_effects=True, vmem_limit_bytes=48 << 20
+            collective_id=0, has_side_effects=True, vmem_limit_bytes=30 << 20
         ),
     )(linv_t, rhs_top, factor_t, rhs_rest)
     return pl.pallas_call(
@@ -452,10 +484,13 @@
             jax.ShapeDtypeStruct(rhs_top.shape, jnp.float32),
             jax.ShapeDtypeStruct(rhs_rest.shape, jnp.float32),
         ),
-        in_specs=[pl.BlockSpec(memory_space=pltpu.VMEM)] * 2,
+        in_specs=[pl.BlockSpec(memory_space=pltpu.VMEM)] * 4,
         out_specs=[pl.BlockSpec(memory_space=pl.ANY)] * 2,
-        scratch_shapes=[pltpu.SemaphoreType.DMA((2,))],
-        compiler_params=pltpu.CompilerParams(vmem_limit_bytes=8 << 20),
+        scratch_shapes=[
+            pltpu.VMEM(rhs_rest.shape, jnp.float32),
+            pltpu.SemaphoreType.DMA((1 + STORE_CUTS,)),
+        ],
+        compiler_params=pltpu.CompilerParams(vmem_limit_bytes=30 << 20),
     )(*(pltpu.with_memory_space_constraint(array, pltpu.VMEM) for array in held))
 
 

time: 102 us -> 89.4 us (0.88)
  Pallas kernels: 101 us -> 87.7 us
    pallas_call x1, Pallas kernels: 96 us -> 82.9 us  [fused_body(): pl.pallas_call(fused_kernel, out_shape=(pltpu.VMEM(rhs_top.shape, jnp.flo...]
where the time goes in v3:
time: 89.4 us; the launch traced here: 88.3 us
  Pallas kernels  87.7 us (98%)
    pallas_call x1, Pallas kernels, fused_body(): pl.pallas_call(fused_kernel, out_shape=(pltpu.VMEM(rhs_top.shape, jnp.flo...  82.9 us
    pallas_call x1, Pallas kernels, fused_body(): pl.pallas_call(store_kernel, out_shape=(jax.ShapeDtypeStruct(rhs_top.shap...  4.77 us

profile of v3, /device:TPU:29, one launch (start us, length us, event | category | flops | bytes accessed | tf_op | source)
XLA Modules:
  0.0 88.3 jit_solution(2767153424958370808)
XLA Ops:
  0.6 82.9 %shard_map.59 = (f32[2,2048,512]{2,1,0:T(8,128)S(1)}, f32[2,1024,512]{2,1,0:T(8,128)S(1)}, bf16[2,2048,1024]{2,1,0:T(8,128)(2,1)S(1)}, bf16[8192,512]{1,0:T(8,128)(2,1)S(1)}) custom-call(bf16[2,64,2048]{2,1,0:T(8,128)(2,1)} %lin_ref.1, f32[2,2048,512]{2,1,0:T(8,128)} %top_ref.1, bf16[2,64,1024]{2,1,0:T(8,128)(2,1)} %fac_ref.1, f32[2,1024,512]{2,1,0:T(8,128)} %rest_ref.1), custom_call_target="tpu_custom_call" | custom-call | tf_op jit(solution)/shard_map/pallas_call | solution.py:461
  83.5 4.8 %shard_map.60 = (f32[2,2048,512]{2,1,0:T(8,128)}, f32[2,1024,512]{2,1,0:T(8,128)}) custom-call(f32[2,2048,512]{2,1,0:T(8,128)S(1)} %get-tuple-element.6.acc, f32[2,1024,512]{2,1,0:T(8,128)S(1)} %get-tuple-element.7.upd, bf16[2,2048,1024]{2,1,0:T(8,128)(2,1)S(1)} %get-tuple-element.8.gfac, bf16[8192,512]{1,0:T(8,128)(2,1)S(1)} %get-tuple-element.9.terms), custom_call_target="tpu_custom_call" | custom-call | tf_op jit(solution)/shard_map/pallas_call | solution.py:481

commit v4 on v3

--- a/solution.py
+++ b/solution.py
@@ -11,32 +11,32 @@
 LEVELS = 4
 PLAN = (
     (
-        516, 129, 130, 532, 776, 529, 530, 66712, 1420, 1541, 1542, 66588,
-        1801, 1558, 1155, 1422, 1421, 1178, 1964, 1802, 1557, 1555, 68668, 3105,
+        516, 129, 130, 532, 776, 529, 530, 33944, 34188, 1541, 1542, 33820,
+        34569, 1558, 1155, 1422, 1421, 1178, 1964, 1802, 1557, 1555, 68668, 3105,
         3106, 69785, 4273, 4495, 4274, 5038, 36893, 38820, 38043, 5150, 5639, 38452,
-        38667, 7085, 6179, 38973, 6679, 40879, 7347, 39967, 12350, 45608, 45621, 12854,
-        242232, 12841, 13222, 12842, 12351, 179109, 14905, 48695, 15930, 81831, 48683, 15931,
-    ),
-    (
-        776, 517, 518, 152, 128, 396, 28, 533, 534, 34569, 1802, 1552,
-        67737, 2446, 2445, 2202, 35335, 34945, 2988, 2077, 2178, 2078, 2108, 3104,
-        36375, 37643, 4625, 4272, 38287, 6062, 38043, 6674, 72621, 7087, 39043, 6175,
-        39998, 7202, 73256, 7201, 7229, 40504, 7346, 7699, 7345, 77734, 44965, 44598,
-        77365, 242218, 78394, 12841, 12323, 13223, 12351, 12855, 114233, 15915, 15539, 15931,
-    ),
-    (
-        396, 28, 777, 778, 516, 153, 154, 397, 1422, 1053, 67614, 2988,
-        2580, 35595, 2108, 2565, 2203, 2566, 2447, 2176, 4014, 35871, 4630, 37397,
-        6061, 38416, 37949, 6063, 37950, 5639, 38018, 5249, 5152, 5655, 71856, 6674,
-        6673, 7076, 39999, 40490, 40500, 7738, 73257, 7202, 7737, 7346, 7299, 8102,
-        7699, 13221, 12321, 45622, 45233, 46635, 46645, 80443, 244771, 49063, 15927, 15539,
-    ),
-    (
-        397, 398, 29, 30, 776, 33944, 1423, 1966, 1965, 1801, 1086, 1055,
-        1085, 1802, 1540, 1178, 34969, 69551, 3851, 3135, 3604, 3589, 3590, 3227,
-        3200, 70166, 4629, 4624, 4615, 5249, 71208, 5655, 105016, 6674, 6673, 72834,
-        7722, 7721, 39968, 7737, 7738, 72880, 7299, 8100, 7699, 7732, 77857, 45611,
-        45233, 13346, 13490, 243622, 46651, 14245, 81461, 15395, 81462, 15539, 15927, 16295,
+        38667, 6061, 6179, 71741, 6679, 7087, 40115, 7199, 39998, 45608, 12853, 12854,
+        242232, 12841, 13222, 12842, 12351, 179109, 14905, 14903, 14906, 81831, 81451, 15931,
+    ),
+    (
+        776, 517, 518, 152, 128, 396, 28, 533, 534, 777, 34570, 1552,
+        67737, 2446, 2445, 2202, 35335, 34945, 2988, 2077, 2178, 2078, 3132, 3104,
+        36375, 3851, 4625, 4272, 71055, 6062, 71835, 6674, 72621, 7087, 6275, 6175,
+        38974, 7202, 106024, 7201, 7229, 7736, 7346, 7699, 7345, 77734, 44965, 44598,
+        110133, 209450, 78394, 12841, 12323, 13223, 12351, 12855, 114233, 15915, 15539, 15931,
+    ),
+    (
+        396, 28, 777, 778, 516, 153, 154, 397, 398, 29, 30, 35756,
+        35348, 35595, 2108, 2565, 2203, 2566, 2447, 2176, 4014, 69663, 37398, 4629,
+        5037, 4624, 4157, 5039, 103486, 5639, 5250, 5249, 5152, 5655, 104624, 6674,
+        6673, 7076, 6207, 6698, 106036, 7738, 40489, 7202, 7737, 7346, 7299, 8102,
+        7699, 13221, 45089, 45622, 45233, 46635, 177717, 147003, 80931, 49063, 15927, 15539,
+    ),
+    (
+        397, 398, 29, 30, 776, 1176, 34191, 1966, 1965, 1801, 1086, 1055,
+        1085, 1802, 1540, 34970, 2201, 2991, 3851, 3135, 69140, 3589, 3590, 3227,
+        3200, 70166, 4629, 4624, 4615, 5249, 38440, 38423, 105016, 6674, 6673, 39042,
+        7722, 40489, 7200, 40505, 40506, 40112, 7299, 8100, 7699, 7732, 45089, 78379,
+        12465, 12322, 46258, 243622, 80443, 15269, 47669, 15395, 81462, 48307, 15927, 16295,
     ),
 )
 ORDER = (
@@ -58,9 +58,9 @@
     ),
 )
 OWN_AT = (8, 30, 30, 2)
-L_CUTS, F_CUTS, TOP_CUTS = 1, 1, 1
+L_CUTS, F_CUTS, TOP_CUTS = 1, 1, 4
 DRAIN = 30
-LEFT = 4
+LEFT = 2
 LATE = 2
 STORE_CUTS = 2
 

time: 89.4 us -> 89.3 us (level)
  no operation moved by 1% of the time
where the time goes in v4:
time: 89.3 us; the launch traced here: 88.2 us
  Pallas kernels  87.6 us (98%)
    pallas_call x1, Pallas kernels, fused_body(): pl.pallas_call(fused_kernel, out_shape=(pltpu.VMEM(rhs_top.shape, jnp.flo...  82.8 us
    pallas_call x1, Pallas kernels, fused_body(): pl.pallas_call(store_kernel, out_shape=(jax.ShapeDtypeStruct(rhs_top.shap...  4.77 us

profile of v4, /device:TPU:29, one launch (start us, length us, event | category | flops | bytes accessed | tf_op | source)
XLA Modules:
  0.0 88.2 jit_solution(4446389944445010423)
XLA Ops:
  0.6 82.8 %shard_map.59 = (f32[2,2048,512]{2,1,0:T(8,128)S(1)}, f32[2,1024,512]{2,1,0:T(8,128)S(1)}, bf16[2,2048,1024]{2,1,0:T(8,128)(2,1)S(1)}, bf16[8192,512]{1,0:T(8,128)(2,1)S(1)}) custom-call(bf16[2,64,2048]{2,1,0:T(8,128)(2,1)} %lin_ref.1, f32[2,2048,512]{2,1,0:T(8,128)} %top_ref.1, bf16[2,64,1024]{2,1,0:T(8,128)(2,1)} %fac_ref.1, f32[2,1024,512]{2,1,0:T(8,128)} %rest_ref.1), custom_call_target="tpu_custom_call" | custom-call | tf_op jit(solution)/shard_map/pallas_call | solution.py:461
  83.5 4.8 %shard_map.60 = (f32[2,2048,512]{2,1,0:T(8,128)}, f32[2,1024,512]{2,1,0:T(8,128)}) custom-call(f32[2,2048,512]{2,1,0:T(8,128)S(1)} %get-tuple-element.6.acc, f32[2,1024,512]{2,1,0:T(8,128)S(1)} %get-tuple-element.7.upd, bf16[2,2048,1024]{2,1,0:T(8,128)(2,1)S(1)} %get-tuple-element.8.gfac, bf16[8192,512]{1,0:T(8,128)(2,1)S(1)} %get-tuple-element.9.terms), custom_call_target="tpu_custom_call" | custom-call | tf_op jit(solution)/shard_map/pallas_call | solution.py:481
